TPU v7x, 32 devices: a whole 2x2x4 slice. The times are simulated.
32 devices in a mesh: seq: 2 (over core), expert: 16 (over z, y, x).
Axes of the slice: x: 2, y: 2, z: 4, core: 2. Of those that a mesh axis runs over, the one named last changes fastest.
Arguments:
- tokens: bfloat16 [4096, 4096], P(('seq', 'expert')), may hold values from -6 to 6
- routes: int32 [4096, 2], P(('seq', 'expert')), may hold values from 0 to 15, all different within a row; in each aligned block of 128 rows (0 to 127, 128 to 255, ...) at most 24 rows name the same one
- route_probs: float32 [4096, 2], P(('seq', 'expert')), may hold values from 0.25 to 1
- gate_weight: bfloat16 [16, 4096, 768], P('expert', None, 'seq'), may hold values from -0.09375 to 0.09375
- up_weight: bfloat16 [16, 4096, 768], P('expert', None, 'seq'), may hold values from -0.09375 to 0.09375
- down_weight: bfloat16 [16, 768, 4096], P('expert', 'seq'), may hold values from -0.21875 to 0.21875
- grad_out: bfloat16 [4096, 4096], P(('seq', 'expert')), may hold values from -3 to 3
Outputs:
- grad_tokens: bfloat16 [4096, 4096], P(('seq', 'expert'))
- grad_probs: bfloat16 [4096, 2], P(('seq', 'expert'))
Inputs may be any that keep to these rules, and one draw needn't show every extreme that they name: `routes`: each token names 2 different experts. Among the tokens of one device no expert is named by more than 24 tokens, and in every draw some device names some expert exactly 24 times.
All inputs are finite; a program needn't handle non-finite values.
Results may differ from a plain program's by a relative error of at most 0.01.
Values may be sent and summed in bfloat16 or wider, within the bound.
A program may use at most 128 MiB of HBM per device.

v0:
```python
import jax
import jax.numpy as jnp
from jax import lax
from jax.sharding import PartitionSpec as P

CHUNKS = 2
NT = (((1,), (1,)), ((), ()))


def dot(a, b):
    return jnp.dot(a, b, preferred_element_type=jnp.float32)


def dot_nt(a, b):
    return lax.dot_general(a, b, NT, preferred_element_type=jnp.float32)


def slots_of(routes, base, half, capacity):
    local = routes - base
    chosen = local.reshape(-1)
    onehot = (chosen[:, None] == jnp.arange(half, dtype=jnp.int32)[None, :]).astype(jnp.int32)
    before = jnp.cumsum(onehot, axis=0) - onehot
    position = jnp.sum(before * onehot, axis=1).reshape(routes.shape)
    valid = (local >= 0) & (local < half)
    return jnp.where(valid, local * capacity + position, -1)


def dispatch_of(slots, count):
    lanes = jnp.arange(count, dtype=jnp.int32)[:, None, None]
    return jnp.any(lanes == slots[None], axis=2).astype(jnp.bfloat16)


def weighting_of(slots, probs, count):
    lanes = jnp.arange(count, dtype=jnp.int32)[None, None, :]
    full = jnp.sum(jnp.where(slots[:, :, None] == lanes, probs[:, :, None], 0.0), axis=1)
    high = lax.reduce_precision(full, 8, 7)
    return high.astype(jnp.bfloat16), (full - high).astype(jnp.bfloat16)


def combine(weighting, rows):
    return dot(weighting[0], rows) + dot(weighting[1], rows)


def pick(slots, values):
    lanes = jnp.arange(values.shape[0], dtype=jnp.int32)[None, None, :]
    return jnp.sum(jnp.where(slots[:, :, None] == lanes, values[None, None, :], 0.0), axis=2)


def front(rows_in, gates, ups):
    return [(dot(rows_in, g), dot(rows_in, u)) for g, u in zip(gates, ups)]


def middle(terms, rows_grad, downs):
    prob, grads = 0.0, []
    for (gating, lifted), d in zip(terms, downs):
        sigmoid = jax.nn.sigmoid(gating)
        active = gating * sigmoid
        hidden = (active * lifted).astype(jnp.bfloat16)
        grad_hidden = dot_nt(rows_grad, d)
        prob = prob + jnp.sum(hidden.astype(jnp.float32) * grad_hidden, axis=1)
        slope_term = sigmoid * (1.0 + gating * (1.0 - sigmoid))
        grads.append(
            (
                (grad_hidden * lifted * slope_term).astype(jnp.bfloat16),
                (grad_hidden * active).astype(jnp.bfloat16),
            )
        )
    return grads, prob


def back(grads, gates, ups, columns):
    total = 0.0
    for (gg, gu), g, u in zip(grads, gates, ups):
        total = total + dot_nt(gg, g[columns]) + dot_nt(gu, u[columns])
    return total.astype(jnp.bfloat16)


def on_device(tokens, routes, route_probs, gate_weight, up_weight, down_weight, grad_out):
    tok_count, width = tokens.shape
    top_count = routes.shape[1]
    experts = lax.axis_size("expert")
    parts = lax.axis_size("seq")
    capacity = 3 * tok_count * top_count // (2 * experts)
    half = experts // 2
    count = half * capacity
    base = (lax.axis_index("expert") // half) * half
    swap = [(i, (i + half) % experts) for i in range(experts)]
    groups = [list(range(half)), list(range(half, experts))]

    def across(value):
        return lax.ppermute(value, "expert", swap)

    def exchange(value):
        value = value.reshape(half, capacity, -1)
        value = lax.all_to_all(
            value, "expert", split_axis=0, concat_axis=0, tiled=True, axis_index_groups=groups
        )
        return value.reshape(count, -1)

    far_routes, far_probs = across(routes), across(route_probs)
    far_tokens, far_grad = across(tokens), across(grad_out)

    gates, ups, downs = [gate_weight[0]], [up_weight[0]], [down_weight[0]]
    for shift in range(1, parts):
        turn = [(i, (i + shift) % parts) for i in range(parts)]
        gates.append(lax.ppermute(gate_weight[0], "seq", turn))
        ups.append(lax.ppermute(up_weight[0], "seq", turn))
        downs.append(lax.ppermute(down_weight[0], "seq", turn))

    near_slots = slots_of(routes, base, half, capacity)
    near_pick = dispatch_of(near_slots, count)
    near_in = exchange(dot(near_pick, tokens).astype(jnp.bfloat16))
    near_out = exchange(dot(near_pick, grad_out).astype(jnp.bfloat16))
    near_grads, near_prob = middle(front(near_in, gates, ups), near_out, downs)

    far_slots = slots_of(far_routes, base, half, capacity)
    far_pick = dispatch_of(far_slots, count)
    far_in = exchange(dot(far_pick, far_tokens).astype(jnp.bfloat16))
    far_terms = front(far_in, gates, ups)
    far_out = exchange(dot(far_pick, far_grad).astype(jnp.bfloat16))
    far_grads, far_prob = middle(far_terms, far_out, downs)

    near_weighting = weighting_of(near_slots, route_probs, count)
    far_weighting = weighting_of(far_slots, far_probs, count)

    size = width // CHUNKS
    spans = [slice(c * size, (c + 1) * size) for c in range(CHUNKS)]

    def send_back(grads, prob, span):
        rows = back(grads, gates, ups, span)
        if span.start == 0:
            column = jnp.broadcast_to(prob.astype(jnp.bfloat16)[:, None], (count, 128))
            rows = jnp.concatenate([rows, column], axis=1)
        return exchange(rows)

    returned = []
    for span in spans:
        rows = send_back(far_grads, far_prob, span)
        partial = combine(far_weighting, rows[:, :size]).astype(jnp.bfloat16)
        returned.append(across(partial))
        if span.start == 0:
            far_values = pick(far_slots, rows[:, size].astype(jnp.float32))
            far_values = across(far_values.astype(jnp.bfloat16))
    pieces = []
    for span, far_piece in zip(spans, returned):
        rows = send_back(near_grads, near_prob, span)
        near_piece = combine(near_weighting, rows[:, :size])
        pieces.append((near_piece + far_piece.astype(jnp.float32)).astype(jnp.bfloat16))
        if span.start == 0:
            near_values = pick(near_slots, rows[:, size].astype(jnp.float32))
    grad_probs = (near_values + far_values.astype(jnp.float32)).astype(jnp.bfloat16)
    return (jnp.concatenate(pieces, axis=1), grad_probs)


def solution(mesh):
    placed = (
        P(("seq", "expert"), None),
        P(("seq", "expert"), None),
        P(("seq", "expert"), None),
        P("expert", None, "seq"),
        P("expert", None, "seq"),
        P("expert", "seq", None),
        P(("seq", "expert"), None),
    )
    return jax.shard_map(
        on_device,
        mesh=mesh,
        in_specs=placed,
        out_specs=(P(("seq", "expert"), None), P(("seq", "expert"), None)),
        check_vma=False,
    )
```

profile of v0, /device:TPU:0, one launch (start us, length us, event | category | flops | bytes accessed | tf_op | source)
XLA Modules:
  0.0 299.5 jit_solution(7705558474026619873)
XLA Ops:
  0.6 0.8 copy.25
  3.0 2.9 convolution_convert_fusion.2
  5.9 6.2 %all-to-all-start.1 = ((bf16[8,24,4096]{2,1,0:T(8,128)(2,1)}), bf16[8,24,4096]{2,1,0:T(8,128)(2,1)S(1)}, u32[]{:S(2)}, u32[]{:S(2)}) async-start(bf16[8,24,4096]{2,1,0:T(8,128)(2,1)} %bitcast.5), calls=%async_computation.1 | async-start | bytes 3145728 | tf_op jit(solution)/shard_map/all_to_all | solution.py:95
  12.1 2.9 convolution_convert_fusion.3
  15.1 17.4 %all-to-all-done.1 = bf16[8,24,4096]{2,1,0:T(8,128)(2,1)S(1)} async-done(((bf16[8,24,4096]{2,1,0:T(8,128)(2,1)}), bf16[8,24,4096]{2,1,0:T(8,128)(2,1)S(1)}, u32[]{:S(2)}, u32[]{:S(2)}) %all-to-all-start.1) | async-done | bytes 1572896 | tf_op jit(solution)/shard_map/all_to_all | solution.py:95
  32.5 1.2 copy-done.8
  33.6 4.3 %all-to-all-start = ((bf16[8,24,4096]{2,1,0:T(8,128)(2,1)}), bf16[8,24,4096]{2,1,0:T(8,128)(2,1)}, u32[]{:S(2)}, u32[]{:S(2)}) async-start(bf16[8,24,4096]{2,1,0:T(8,128)(2,1)} %bitcast.2), calls=%async_computation | async-start | bytes 3145728 | tf_op jit(solution)/shard_map/all_to_all | solution.py:95
  37.9 2.7 collective-permute-start.6
  40.9 2.6 collective-permute-start.5
  44.0 68.9 %collective-permute-done.3 = s32[128,2]{1,0:T(8,128)S(1)} collective-permute-done((s32[128,2]{1,0:T(8,128)S(1)}, s32[128,2]{1,0:T(8,128)S(1)}, u32[]{:S(2)}, u32[]{:S(2)}) %collective-permute-start.3) | collective-permute-done | bytes 1056 | tf_op jit(solution)/shard_map/ppermute | solution.py:91
  114.4 3.1 %convolution_convert_fusion = bf16[192,4096]{1,0:T(8,128)(2,1)} fusion(pred[192,128]{1,0:T(8,128)(4,1)S(1)} %fusion.55, bf16[128,4096]{1,0:T(8,128)(2,1)} %collective-permute-done.6), kind=kOutput, calls=%fused_computation | convolution fusion | flops 202113024 | bytes 2646016 | tf_op jit(solution)/shard_map/dot_general | solution.py:11
  117.6 16.2 %collective-permute-done.5 = bf16[128,4096]{1,0:T(8,128)(2,1)} collective-permute-done((bf16[128,4096]{1,0:T(8,128)(2,1)}, bf16[128,4096]{1,0:T(8,128)(2,1)}, u32[]{:S(2)}, u32[]{:S(2)}) %collective-permute-start.5) | collective-permute-done | bytes 1048608 | tf_op jit(solution)/shard_map/ppermute | solution.py:91
  133.8 2.9 convolution_convert_fusion.1
  136.8 1.0 fusion.72
  137.7 4.3 %all-to-all-start.4 = ((bf16[8,24,4096]{2,1,0:T(8,128)(2,1)}), bf16[8,24,4096]{2,1,0:T(8,128)(2,1)}, u32[]{:S(2)}, u32[]{:S(2)}) async-start(bf16[8,24,4096]{2,1,0:T(8,128)(2,1)} %bitcast.126), calls=%async_computation.4 | async-start | bytes 3145728 | tf_op jit(solution)/shard_map/all_to_all | solution.py:95
  142.1 3.5 %fusion.76 = f32[192,384]{1,0:T(8,128)S(1)} fusion(bf16[192,4096]{1,0:T(8,128)(2,1)} %bitcast.119, bf16[1,4096,384]{2,1,0:T(8,128)(2,1)} %param.11), kind=kOutput, calls=%fused_computation.140 | convolution fusion | flops 603979776 | bytes 5013504 | tf_op jit(solution)/shard_map/dot_general | solution.py:11
  145.6 2.9 multiply_reduce_fusion.3
  149.9 1.2 copy-done.4
  151.1 1.9 convolution_add_fusion.7
  153.0 1.9 convolution_add_fusion.3
  154.8 1.0 fusion.82
  155.9 3.6 %fusion.83 = f32[192,384]{1,0:T(8,128)} fusion(bf16[192,4096]{1,0:T(8,128)(2,1)S(1)} %bitcast.122, bf16[4096,384]{1,0:T(8,128)(2,1)} %collective-permute-done.2), kind=kOutput, calls=%fused_computation.147 | convolution fusion | flops 603979776 | bytes 5013504 | tf_op jit(solution)/shard_map/dot_general | solution.py:11
  159.5 2.1 all-to-all-done.4
  161.6 4.5 %all-to-all-start.3 = ((bf16[8,24,4096]{2,1,0:T(8,128)(2,1)}), bf16[8,24,4096]{2,1,0:T(8,128)(2,1)}, u32[]{:S(2)}, u32[]{:S(2)}) async-start(bf16[8,24,4096]{2,1,0:T(8,128)(2,1)} %bitcast.125), calls=%async_computation.3 | async-start | bytes 3145728 | tf_op jit(solution)/shard_map/all_to_all | solution.py:95
  166.1 3.8 %multiply_reduce_fusion.2 = (f32[192]{0:T(256)S(1)}, bf16[192,384]{1,0:T(8,128)(2,1)S(1)}, bf16[192,384]{1,0:T(8,128)(2,1)S(1)}) fusion(f32[192,384]{1,0:T(8,128)S(1)} %fusion.82, f32[192,384]{1,0:T(8,128)} %fusion.83, bf16[192,4096]{1,0:T(8,128)(2,1)} %bitcast.3, bf16[384,4096]{1,0:T(8,128)(2,1)} %collective-permute-done), kind=kOutput, calls=%fused_computation.81 | convolution fusion | flops 605306688 | bytes 5604096 | tf_op jit(solution)/shard_map/dot_general | solution.py:15
  169.9 0.7 fusion.30
  170.6 0.7 fusion.24
  172.0 2.1 fusion.4
  174.3 1.0 pad_maximum_fusion.1
  175.9 3.2 %fusion.6 = bf16[192,2048]{1,0:T(8,128)(2,1)} fusion(f32[192,2048]{1,0:T(8,128)S(1)} %fusion.24, f32[192,2048]{1,0:T(8,128)S(1)} %copy-done.11, bf16[192,384]{1,0:T(8,128)(2,1)S(1)} %get-tuple-element.11, bf16[4096,384]{1,0:T(8,128)(2,1)} %collective-permute-done.2), kind=kOutput, calls=%fused_computation.18 | convolution fusion | flops 303169536 | bytes 5652480 | tf_op jit(solution)/shard_map/dot_general | solution.py:15
  179.1 3.3 %fusion.70 = f32[192,384]{1,0:T(8,128)} fusion(bf16[192,4096]{1,0:T(8,128)(2,1)} %bitcast.18, bf16[1,4096,384]{2,1,0:T(8,128)(2,1)S(1)} %copy-done.2), kind=kOutput, calls=%fused_computation.134 | convolution fusion | flops 603979776 | bytes 5013504 | tf_op jit(solution)/shard_map/dot_general | solution.py:11
  182.4 3.1 %fusion.74 = f32[192,384]{1,0:T(8,128)} fusion(bf16[192,4096]{1,0:T(8,128)(2,1)} %bitcast.18, bf16[1,4096,384]{2,1,0:T(8,128)(2,1)S(1)} %copy-done.5), kind=kOutput, calls=%fused_computation.138 | convolution fusion | flops 603979776 | bytes 5013504 | tf_op jit(solution)/shard_map/dot_general | solution.py:11
  185.9 4.4 %all-to-all-start.6 = ((bf16[8,24,2048]{2,1,0:T(8,128)(2,1)}), bf16[8,24,2048]{2,1,0:T(8,128)(2,1)}, u32[]{:S(2)}, u32[]{:S(2)}) async-start(bf16[8,24,2048]{2,1,0:T(8,128)(2,1)} %bitcast.129), calls=%async_computation.6 | async-start | bytes 1572864 | tf_op jit(solution)/shard_map/all_to_all | solution.py:95
  190.4 3.9 %multiply_reduce_fusion.1 = (f32[192]{0:T(256)S(1)}, bf16[192,384]{1,0:T(8,128)(2,1)S(1)}, bf16[192,384]{1,0:T(8,128)(2,1)S(1)}) fusion(f32[192,384]{1,0:T(8,128)} %fusion.74, f32[192,384]{1,0:T(8,128)} %fusion.70, bf16[192,4096]{1,0:T(8,128)(2,1)} %bitcast.16, bf16[1,384,4096]{2,1,0:T(8,128)(2,1)} %param.12), kind=kOutput, calls=%fused_computation.71 | convolution fusion | flops 605306688 | bytes 5604096 | tf_op jit(solution)/shard_map/dot_general | solution.py:15
  194.3 1.9 fusion.18
  196.2 2.4 fusion.84
  198.6 3.3 %fusion.85 = f32[192,384]{1,0:T(8,128)S(1)} fusion(bf16[192,4096]{1,0:T(8,128)(2,1)} %bitcast.18, bf16[4096,384]{1,0:T(8,128)(2,1)} %collective-permute-done.2), kind=kOutput, calls=%fused_computation.149 | convolution fusion | flops 603979776 | bytes 5013504 | tf_op jit(solution)/shard_map/dot_general | solution.py:11
  202.0 4.3 %multiply_reduce_fusion = (f32[192]{0:T(256)S(1)}, bf16[192,384]{1,0:T(8,128)(2,1)}, bf16[192,384]{1,0:T(8,128)(2,1)}) fusion(f32[192,384]{1,0:T(8,128)S(1)} %fusion.84, f32[192,384]{1,0:T(8,128)S(1)} %fusion.85, bf16[192,4096]{1,0:T(8,128)(2,1)} %bitcast.16, bf16[384,4096]{1,0:T(8,128)(2,1)} %collective-permute-done), kind=kOutput, calls=%fused_computation.69 | convolution fusion | flops 605306688 | bytes 5604096 | tf_op jit(solution)/shard_map/dot_general | solution.py:15
  206.3 5.1 %all-to-all-start.2 = ((bf16[8,24,2176]{2,1,0:T(8,128)(2,1)}), bf16[8,24,2176]{2,1,0:T(8,128)(2,1)}, u32[]{:S(2)}, u32[]{:S(2)}) async-start(bf16[8,24,2176]{2,1,0:T(8,128)(2,1)} %bitcast.127), calls=%async_computation.2 | async-start | bytes 1671168 | tf_op jit(solution)/shard_map/all_to_all | solution.py:95
  211.4 1.8 fusion.28
  213.4 2.2 convolution_add_fusion.5
  215.6 2.1 fusion.5
  217.8 1.0 pad_maximum_fusion.2
  218.8 3.8 %all-to-all-done.2 = bf16[8,24,2176]{2,1,0:T(8,128)(2,1)} async-done(((bf16[8,24,2176]{2,1,0:T(8,128)(2,1)}), bf16[8,24,2176]{2,1,0:T(8,128)(2,1)}, u32[]{:S(2)}, u32[]{:S(2)}) %all-to-all-start.2) | async-done | bytes 835616 | tf_op jit(solution)/shard_map/all_to_all | solution.py:95
  222.6 4.4 %all-to-all-start.5 = ((bf16[8,24,2176]{2,1,0:T(8,128)(2,1)}), bf16[8,24,2176]{2,1,0:T(8,128)(2,1)}, u32[]{:S(2)}, u32[]{:S(2)}) async-start(bf16[8,24,2176]{2,1,0:T(8,128)(2,1)} %bitcast.128), calls=%async_computation.5 | async-start | bytes 1671168 | tf_op jit(solution)/shard_map/all_to_all | solution.py:95
  227.1 2.9 collective-permute-start.4
  230.0 2.1 fusion.12
  232.8 1.2 copy-done.7
  234.0 0.7 convolution_add_fusion.1
  234.9 3.0 %fusion.7 = bf16[192,2048]{1,0:T(8,128)(2,1)} fusion(f32[192,2048]{1,0:T(8,128)S(1)} %fusion.22, f32[192,2048]{1,0:T(8,128)S(1)} %convolution_add_fusion.1, bf16[192,384]{1,0:T(8,128)(2,1)S(1)} %copy-done.14, bf16[4096,384]{1,0:T(8,128)(2,1)} %collective-permute-done.2), kind=kOutput, calls=%fused_computation.19 | convolution fusion | flops 303169536 | bytes 5652480 | tf_op jit(solution)/shard_map/dot_general | solution.py:15
  237.9 0.9 convert_reduce_fusion.1
  238.8 4.8 %all-to-all-start.7 = ((bf16[8,24,2048]{2,1,0:T(8,128)(2,1)}), bf16[8,24,2048]{2,1,0:T(8,128)(2,1)S(1)}, u32[]{:S(2)}, u32[]{:S(2)}) async-start(bf16[8,24,2048]{2,1,0:T(8,128)(2,1)} %bitcast.25), calls=%async_computation.7 | async-start | bytes 1572864 | tf_op jit(solution)/shard_map/all_to_all | solution.py:95
  243.7 1.5 fusion.58
  245.2 1.5 convolution_add_fusion.9
  246.7 0.9 convert_reduce_fusion
  248.4 1.5 fusion.43
  249.9 1.5 fusion.8
  251.3 2.3 collective-permute-start.7
  254.4 1.7 collective-permute-start.8
  256.0 1.5 fusion.46
  258.0 30.4 %collective-permute-done.7 = bf16[128,2048]{1,0:T(8,128)(2,1)S(1)} collective-permute-done((bf16[128,2048]{1,0:T(8,128)(2,1)S(1)}, bf16[128,2048]{1,0:T(8,128)(2,1)S(1)}, u32[]{:S(2)}, u32[]{:S(2)}) %collective-permute-start.7) | collective-permute-done | bytes 524320 | tf_op jit(solution)/shard_map/ppermute | solution.py:91
  288.4 1.5 add_convert_fusion.1
  289.9 8.5 %collective-permute-done.8 = bf16[128,2048]{1,0:T(8,128)(2,1)S(1)} collective-permute-done((bf16[128,2048]{1,0:T(8,128)(2,1)S(1)}, bf16[128,2048]{1,0:T(8,128)(2,1)S(1)}, u32[]{:S(2)}, u32[]{:S(2)}) %collective-permute-start.8) | collective-permute-done | bytes 524320 | tf_op jit(solution)/shard_map/ppermute | solution.py:91
  298.5 1.1 pad_maximum_fusion
  (88 shorter events, 10.5 us)
Async XLA Ops:
  5.9 26.5 %all-to-all-start.1 = ((bf16[8,24,4096]{2,1,0:T(8,128)(2,1)}), bf16[8,24,4096]{2,1,0:T(8,128)(2,1)S(1)}, u32[]{:S(2)}, u32[]{:S(2)}) async-start(bf16[8,24,4096]{2,1,0:T(8,128)(2,1)} %bitcast.5), calls=%async_computation.1 | async-start | bytes 3145728 | tf_op jit(solution)/shard_map/all_to_all | solution.py:95
  32.5 1.2 copy-start.8
  33.6 104.1 %all-to-all-start = ((bf16[8,24,4096]{2,1,0:T(8,128)(2,1)}), bf16[8,24,4096]{2,1,0:T(8,128)(2,1)}, u32[]{:S(2)}, u32[]{:S(2)}) async-start(bf16[8,24,4096]{2,1,0:T(8,128)(2,1)} %bitcast.2), calls=%async_computation | async-start | bytes 3145728 | tf_op jit(solution)/shard_map/all_to_all | solution.py:95
  37.9 76.5 %collective-permute-start.6 = (bf16[128,4096]{1,0:T(8,128)(2,1)}, bf16[128,4096]{1,0:T(8,128)(2,1)}, u32[]{:S(2)}, u32[]{:S(2)}) collective-permute-start(bf16[128,4096]{1,0:T(8,128)(2,1)} %param.7), channel_id=1, source_target_pairs={{0,8},{1,9},{2,10},{3,11},{4,12},{5,13},{6,14},{7,15},{8,0},{9,1},... | collective-permute-start | bytes 3145736 | tf_op jit(solution)/shard_map/ppermute | solution.py:91
  40.6 72.3 %collective-permute-start.3 = (s32[128,2]{1,0:T(8,128)S(1)}, s32[128,2]{1,0:T(8,128)S(1)}, u32[]{:S(2)}, u32[]{:S(2)}) collective-permute-start(s32[128,2]{1,0:T(8,128)S(1)} %copy.25), channel_id=1, source_target_pairs={{0,8},{1,9},{2,10},{3,11},{4,12},{5,13},{6,14},{7,15},{8,0},{9,1},... | collective-permute-start | bytes 3080 | tf_op jit(solution)/shard_map/ppermute | solution.py:91
  40.9 92.9 %collective-permute-start.5 = (bf16[128,4096]{1,0:T(8,128)(2,1)}, bf16[128,4096]{1,0:T(8,128)(2,1)}, u32[]{:S(2)}, u32[]{:S(2)}) collective-permute-start(bf16[128,4096]{1,0:T(8,128)(2,1)} %param.13), channel_id=1, source_target_pairs={{0,8},{1,9},{2,10},{3,11},{4,12},{5,13},{6,14},{7,15},{8,0},{9,1},... | collective-permute-start | bytes 3145736 | tf_op jit(solution)/shard_map/ppermute | solution.py:91
  43.5 111.3 %collective-permute-start.1 = (bf16[4096,384]{1,0:T(8,128)(2,1)}, bf16[4096,384]{1,0:T(8,128)(2,1)S(1)}, u32[]{:S(2)}, u32[]{:S(2)}) collective-permute-start(bf16[4096,384]{1,0:T(8,128)(2,1)} %bitcast.118), channel_id=1, source_target_pairs={{0,16},{16,0},{1,17},{17,1},{2,18},{18,2},{3,19},{19,3},{4,20},{20... | collective-permute-start | bytes 9437192 | tf_op jit(solution)/shard_map/ppermute | solution.py:107
  43.5 112.3 %collective-permute-start.2 = (bf16[4096,384]{1,0:T(8,128)(2,1)}, bf16[4096,384]{1,0:T(8,128)(2,1)}, u32[]{:S(2)}, u32[]{:S(2)}) collective-permute-start(bf16[4096,384]{1,0:T(8,128)(2,1)} %bitcast.117), channel_id=1, source_target_pairs={{0,16},{16,0},{1,17},{17,1},{2,18},{18,2},{3,19},{19,3},{4,20},{20... | collective-permute-start | bytes 9437192 | tf_op jit(solution)/shard_map/ppermute | solution.py:106
  112.9 53.2 %collective-permute-start = (bf16[384,4096]{1,0:T(8,128)(2,1)}, bf16[384,4096]{1,0:T(8,128)(2,1)}, u32[]{:S(2)}, u32[]{:S(2)}) collective-permute-start(bf16[384,4096]{1,0:T(8,128)(2,1)} %bitcast.130), channel_id=1, source_target_pairs={{0,16},{16,0},{1,17},{17,1},{2,18},{18,2},{3,19},{19,3},{4,20},{20... | collective-permute-start | bytes 9437192 | tf_op jit(solution)/shard_map/ppermute | solution.py:108
  114.4 22.3 %copy-start = (bf16[1,4096,384]{2,1,0:T(8,128)(2,1)S(1)}, bf16[1,4096,384]{2,1,0:T(8,128)(2,1)}, u32[]{:S(2)}) copy-start(bf16[1,4096,384]{2,1,0:T(8,128)(2,1)} %param.10) | copy-start | bytes 9437188
  117.6 19.2 %copy-start.9 = (bf16[8,24,4096]{2,1,0:T(8,128)(2,1)S(1)}, bf16[8,24,4096]{2,1,0:T(8,128)(2,1)}, u32[]{:S(2)}) copy-start(bf16[8,24,4096]{2,1,0:T(8,128)(2,1)} %copy-done.8) | copy-start | bytes 4718596
  137.7 23.8 %all-to-all-start.4 = ((bf16[8,24,4096]{2,1,0:T(8,128)(2,1)}), bf16[8,24,4096]{2,1,0:T(8,128)(2,1)}, u32[]{:S(2)}, u32[]{:S(2)}) async-start(bf16[8,24,4096]{2,1,0:T(8,128)(2,1)} %bitcast.126), calls=%async_computation.4 | async-start | bytes 3145728 | tf_op jit(solution)/shard_map/all_to_all | solution.py:95
  142.1 3.5 %copy-start.17 = (bf16[1,384,4096]{2,1,0:T(8,128)(2,1)S(1)}, bf16[1,384,4096]{2,1,0:T(8,128)(2,1)}, u32[]{:S(2)}) copy-start(bf16[1,384,4096]{2,1,0:T(8,128)(2,1)} %param.12) | copy-start | bytes 9437188
  145.6 2.9 copy-start.1
  149.2 1.9 copy-start.4
  153.0 1.9 copy-start.10
  161.6 24.4 %all-to-all-start.3 = ((bf16[8,24,4096]{2,1,0:T(8,128)(2,1)}), bf16[8,24,4096]{2,1,0:T(8,128)(2,1)}, u32[]{:S(2)}, u32[]{:S(2)}) async-start(bf16[8,24,4096]{2,1,0:T(8,128)(2,1)} %bitcast.125), calls=%async_computation.3 | async-start | bytes 3145728 | tf_op jit(solution)/shard_map/all_to_all | solution.py:95
  170.6 1.4 copy-start.12
  174.2 1.7 copy-start.11
  175.9 3.2 %copy-start.2 = (bf16[1,4096,384]{2,1,0:T(8,128)(2,1)S(1)}, bf16[1,4096,384]{2,1,0:T(8,128)(2,1)}, u32[]{:S(2)}) copy-start(bf16[1,4096,384]{2,1,0:T(8,128)(2,1)} %param.10) | copy-start | bytes 9437188
  179.1 3.3 %copy-start.5 = (bf16[1,4096,384]{2,1,0:T(8,128)(2,1)S(1)}, bf16[1,4096,384]{2,1,0:T(8,128)(2,1)}, u32[]{:S(2)}) copy-start(bf16[1,4096,384]{2,1,0:T(8,128)(2,1)} %param.11) | copy-start | bytes 9437188
  185.9 20.4 %all-to-all-start.6 = ((bf16[8,24,2048]{2,1,0:T(8,128)(2,1)}), bf16[8,24,2048]{2,1,0:T(8,128)(2,1)}, u32[]{:S(2)}, u32[]{:S(2)}) async-start(bf16[8,24,2048]{2,1,0:T(8,128)(2,1)} %bitcast.129), calls=%async_computation.6 | async-start | bytes 1572864 | tf_op jit(solution)/shard_map/all_to_all | solution.py:95
  190.3 4.0 %copy-start.3 = (bf16[1,4096,384]{2,1,0:T(8,128)(2,1)S(1)}, bf16[1,4096,384]{2,1,0:T(8,128)(2,1)}, u32[]{:S(2)}) copy-start(bf16[1,4096,384]{2,1,0:T(8,128)(2,1)} %param.10) | copy-start | bytes 9437188
  206.3 16.3 %all-to-all-start.2 = ((bf16[8,24,2176]{2,1,0:T(8,128)(2,1)}), bf16[8,24,2176]{2,1,0:T(8,128)(2,1)}, u32[]{:S(2)}, u32[]{:S(2)}) async-start(bf16[8,24,2176]{2,1,0:T(8,128)(2,1)} %bitcast.127), calls=%async_computation.2 | async-start | bytes 1671168 | tf_op jit(solution)/shard_map/all_to_all | solution.py:95
  211.4 2.0 copy-start.6
  213.4 2.2 copy-start.13
  217.8 9.3 %copy-start.16 = (f32[128,2]{0,1:T(2,128)S(1)}, f32[128,2]{0,1:T(2,128)}, u32[]{:S(2)}) copy-start(f32[128,2]{0,1:T(2,128)} %param.9) | copy-start | bytes 3076
  222.6 16.2 %all-to-all-start.5 = ((bf16[8,24,2176]{2,1,0:T(8,128)(2,1)}), bf16[8,24,2176]{2,1,0:T(8,128)(2,1)}, u32[]{:S(2)}, u32[]{:S(2)}) async-start(bf16[8,24,2176]{2,1,0:T(8,128)(2,1)} %bitcast.128), calls=%async_computation.5 | async-start | bytes 1671168 | tf_op jit(solution)/shard_map/all_to_all | solution.py:95
  227.1 5.1 %copy-start.15 = (bf16[192,384]{1,0:T(8,128)(2,1)S(1)}, bf16[192,384]{1,0:T(8,128)(2,1)}, u32[]{:S(2)}) copy-start(bf16[192,384]{1,0:T(8,128)(2,1)} %get-tuple-element.14) | copy-start | bytes 442372
  227.1 20.5 %collective-permute-start.4 = (f32[128,2]{0,1:T(2,128)S(1)}, f32[128,2]{0,1:T(2,128)S(1)}, u32[]{:S(2)}, u32[]{:S(2)}) collective-permute-start(f32[128,2]{0,1:T(2,128)S(1)} %copy-done.16), channel_id=1, source_target_pairs={{0,8},{1,9},{2,10},{3,11},{4,12},{5,13},{6,14},{7,15},{8,0},{9,1},... | collective-permute-start | bytes 3080 | tf_op jit(solution)/shard_map/ppermute | solution.py:91
  232.1 1.9 copy-start.7
  234.0 0.9 copy-start.14
  238.8 14.8 %all-to-all-start.7 = ((bf16[8,24,2048]{2,1,0:T(8,128)(2,1)}), bf16[8,24,2048]{2,1,0:T(8,128)(2,1)S(1)}, u32[]{:S(2)}, u32[]{:S(2)}) async-start(bf16[8,24,2048]{2,1,0:T(8,128)(2,1)} %bitcast.25), calls=%async_computation.7 | async-start | bytes 1572864 | tf_op jit(solution)/shard_map/all_to_all | solution.py:95
  247.7 9.8 %collective-permute-start.9 = (bf16[128,2]{0,1:T(2,128)(2,1)S(1)}, bf16[128,2]{0,1:T(2,128)(2,1)S(1)}, u32[]{:S(2)}, u32[]{:S(2)}) collective-permute-start(bf16[128,2]{0,1:T(2,128)(2,1)S(1)} %get-tuple-element.2), channel_id=1, source_target_pairs={{0,8},{1,9},{2,10},{3,11},{4,12},{5,13},{6,14},{7,15},{8,0},{9,1},... | collective-permute-start | bytes 1544 | tf_op jit(solution)/shard_map/ppermute | solution.py:91
  251.3 37.1 %collective-permute-start.7 = (bf16[128,2048]{1,0:T(8,128)(2,1)S(1)}, bf16[128,2048]{1,0:T(8,128)(2,1)S(1)}, u32[]{:S(2)}, u32[]{:S(2)}) collective-permute-start(bf16[128,2048]{1,0:T(8,128)(2,1)S(1)} %fusion.8), channel_id=1, source_target_pairs={{0,8},{1,9},{2,10},{3,11},{4,12},{5,13},{6,14},{7,15},{8,0},{9,1},... | collective-permute-start | bytes 1572872 | tf_op jit(solution)/shard_map/ppermute | solution.py:91
  254.4 44.0 %collective-permute-start.8 = (bf16[128,2048]{1,0:T(8,128)(2,1)S(1)}, bf16[128,2048]{1,0:T(8,128)(2,1)S(1)}, u32[]{:S(2)}, u32[]{:S(2)}) collective-permute-start(bf16[128,2048]{1,0:T(8,128)(2,1)S(1)} %fusion.9), channel_id=1, source_target_pairs={{0,8},{1,9},{2,10},{3,11},{4,12},{5,13},{6,14},{7,15},{8,0},{9,1},... | collective-permute-start | bytes 1572872 | tf_op jit(solution)/shard_map/ppermute | solution.py:91
where the time goes:
time: 301 us; the launch traced here: 300 us
  waiting for transfers between devices  148 us (49%)
  matrix products  84 us (28%)
  starting transfers between devices  51.7 us (17%)
  local copies, waits for them, and re-layouts  7.63 us (3%)
  other arithmetic  7.3 us (2%)
    ppermute x7, waiting for transfers between devices, across(): return lax.ppermute(value, 'expert', swap)  124 us
    dot_general x20, matrix products, dot(): return jnp.dot(a, b, preferred_element_type=jnp.float32)  42.7 us
    dot_general x20, matrix products, dot_nt(): return lax.dot_general(a, b, NT, preferred_element_type=jnp.float32)  41.4 us
    all_to_all x8, starting transfers between devices, exchange(): lax.all_to_all(value, 'expert', split_axis=0, concat_axis=0, tiled=True,...  38 us
    all_to_all x8, waiting for transfers between devices, exchange(): lax.all_to_all(value, 'expert', split_axis=0, concat_axis=0, tiled=True,...  23.7 us
    ppermute x7, starting transfers between devices, across(): return lax.ppermute(value, 'expert', swap)  13.2 us
    unnamed x37, local copies, waits for them, and re-layouts  6.07 us
  transfers between devices with their start and end apart: 18, of which 8 were waited for; matrix products, arithmetic and copies ran while one was open for 29% of the time, Pallas kernels for 0%

commit v1 on v0

--- a/solution.py
+++ b/solution.py
@@ -1,9 +1,14 @@
 import jax
 import jax.numpy as jnp
 from jax import lax
+from jax.experimental import pallas as pl
+from jax.experimental.pallas import tpu as pltpu
 from jax.sharding import PartitionSpec as P
 
 CHUNKS = 2
+PIECES = 4
+STEP = 512
+MESH = pl.DeviceIdType.MESH
 NT = (((1,), (1,)), ((), ()))
 
 
@@ -75,7 +80,7 @@
     return total.astype(jnp.bfloat16)
 
 
-def on_device(tokens, routes, route_probs, gate_weight, up_weight, down_weight, grad_out):
+def halves_on_device(tokens, routes, route_probs, gate_weight, up_weight, down_weight, grad_out):
     tok_count, width = tokens.shape
     top_count = routes.shape[1]
     experts = lax.axis_size("expert")
@@ -152,6 +157,324 @@
     return (jnp.concatenate(pieces, axis=1), grad_probs)
 
 
+def fused_kernel(
+    half,
+    tokens, grads, near_pick, far_pick_out, near_mats, far_mats_out, gate_hbm, up_hbm, down_hbm,
+    out, probs_out,
+    far_pick, far_mats, far_tok, gate_w, up_w, down_w, send, recv, acc, grad_hid,
+    back_send, back_recv, prob_send, prob_recv, part_send, part_recv, val_send, val_recv,
+    local_sem, x_send, x_recv, w_send, w_recv, a_send, a_recv, b_send, b_recv, p_send, p_recv,
+    y_send, y_recv, v_send, v_recv,
+):
+    tok_count, width = tokens.shape
+    capacity = send.shape[2]
+    count = half * capacity
+    hid = acc.shape[3]
+    piece = width // PIECES
+    me = lax.axis_index("expert")
+    core = lax.axis_index("seq")
+    base = (me // half) * half
+    mine = me - base
+    partner = {"expert": lax.rem(me + half, 2 * half)}
+    twin = {"seq": 1 - core}
+    peers = [lax.rem(mine + d, half) for d in range(half)]
+
+    def remote(src, dst, ss, rs, device):
+        return pltpu.make_async_remote_copy(
+            src_ref=src, dst_ref=dst, send_sem=ss, recv_sem=rs,
+            device_id=device, device_id_type=MESH,
+        )
+
+    locals_ = [
+        pltpu.make_async_copy(src.at[0], dst.at[0], local_sem.at[i])
+        for i, (src, dst) in enumerate(((gate_hbm, gate_w), (up_hbm, up_w), (down_hbm, down_w)))
+    ]
+    for copy in locals_:
+        copy.start()
+
+    barrier = pltpu.get_barrier_semaphore()
+    pl.semaphore_signal(barrier, inc=1, device_id=partner, device_id_type=MESH)
+    pl.semaphore_signal(barrier, inc=1, device_id=twin, device_id_type=MESH)
+    for d in range(1, half):
+        pl.semaphore_signal(
+            barrier, inc=1, device_id={"expert": base + peers[d]}, device_id_type=MESH
+        )
+    pl.semaphore_wait(barrier, half + 1)
+
+    crossing = [
+        remote(far_pick_out, far_pick, x_send.at[0], x_recv.at[0], partner),
+        remote(tokens, far_tok.at[0], x_send.at[1], x_recv.at[1], partner),
+        remote(grads, far_tok.at[1], x_send.at[2], x_recv.at[2], partner),
+        remote(far_mats_out, far_mats, x_send.at[3], x_recv.at[3], partner),
+    ]
+    for copy in crossing:
+        copy.start()
+    swaps = [
+        remote(src.at[0], dst.at[1], w_send.at[i], w_recv.at[i], twin)
+        for i, (src, dst) in enumerate(((gate_hbm, gate_w), (up_hbm, up_w), (down_hbm, down_w)))
+    ]
+    for copy in swaps:
+        copy.start()
+
+    def dispatch(pick, source, stream):
+        @pl.loop(0, width // STEP)
+        def _(k):
+            cols = pl.ds(pl.multiple_of(k * STEP, STEP), STEP)
+            rows = dot(pick[...], source[:, cols])
+            send[stream, :, :, cols] = rows.reshape(half, capacity, STEP).astype(jnp.bfloat16)
+
+        copies = [
+            remote(
+                send.at[stream, peers[d]], recv.at[stream, mine],
+                a_send.at[stream, d], a_recv.at[stream, d], {"expert": base + peers[d]},
+            )
+            for d in range(1, half)
+        ]
+        for copy in copies:
+            copy.start()
+        recv[stream, mine] = send[stream, mine]
+        return copies
+
+    def rows_of(buffer, cols):
+        block = buffer[:, :, cols].astype(jnp.float32)
+        return block.reshape(count, block.shape[2]).astype(jnp.bfloat16)
+
+    def front_in(stream):
+        acc[0] = jnp.zeros(acc.shape[1:], jnp.float32)
+        acc[1] = jnp.zeros(acc.shape[1:], jnp.float32)
+
+        @pl.loop(0, width // STEP)
+        def _(k):
+            cols = pl.ds(pl.multiple_of(k * STEP, STEP), STEP)
+            rows = rows_of(recv.at[stream], cols)
+            for j in range(2):
+                acc[0, j] += dot(rows, gate_w[j, cols, :])
+                acc[1, j] += dot(rows, up_w[j, cols, :])
+
+    def front_out(stream):
+        acc[2] = jnp.zeros(acc.shape[1:], jnp.float32)
+
+        @pl.loop(0, width // STEP)
+        def _(k):
+            cols = pl.ds(pl.multiple_of(k * STEP, STEP), STEP)
+            rows = rows_of(recv.at[stream], cols)
+            for j in range(2):
+                acc[2, j] += dot_nt(rows, down_w[j, :, cols])
+
+    def pointwise(which):
+        prob = jnp.zeros((count, 1), jnp.float32)
+        for j in range(2):
+            gating, lifted, grad_hidden = acc[0, j], acc[1, j], acc[2, j]
+            sigmoid = jax.nn.sigmoid(gating)
+            active = gating * sigmoid
+            hidden = (active * lifted).astype(jnp.bfloat16)
+            prob += jnp.sum(hidden.astype(jnp.float32) * grad_hidden, axis=1, keepdims=True)
+            slope_term = sigmoid * (1.0 + gating * (1.0 - sigmoid))
+            grad_hid[which, 0, j] = (grad_hidden * lifted * slope_term).astype(jnp.bfloat16)
+            grad_hid[which, 1, j] = (grad_hidden * active).astype(jnp.bfloat16)
+        wide = jnp.broadcast_to(prob, (count, 128)).reshape(half, capacity, 128)
+        prob_send[which] = wide.astype(jnp.bfloat16)
+
+    def return_probs(which):
+        copies = [
+            remote(
+                prob_send.at[which, peers[d]], prob_recv.at[which, mine],
+                p_send.at[which, d], p_recv.at[which, d], {"expert": base + peers[d]},
+            )
+            for d in range(1, half)
+        ]
+        for copy in copies:
+            copy.start()
+        prob_recv[which, mine] = prob_send[which, mine]
+        return copies
+
+    def return_rows(which, c):
+        @pl.loop(0, piece // STEP)
+        def _(k):
+            cols = pl.ds(pl.multiple_of(c * piece + k * STEP, STEP), STEP)
+            total = dot_nt(grad_hid[which, 0, 0], gate_w[0, cols, :])
+            total += dot_nt(grad_hid[which, 0, 1], gate_w[1, cols, :])
+            total += dot_nt(grad_hid[which, 1, 0], up_w[0, cols, :])
+            total += dot_nt(grad_hid[which, 1, 1], up_w[1, cols, :])
+            inner = pl.ds(pl.multiple_of(k * STEP, STEP), STEP)
+            back_send[which, c, :, :, inner] = total.reshape(half, capacity, STEP).astype(
+                jnp.bfloat16
+            )
+
+        copies = [
+            remote(
+                back_send.at[which, c, peers[d]], back_recv.at[which, c, mine],
+                b_send.at[which, c, d], b_recv.at[which, c, d], {"expert": base + peers[d]},
+            )
+            for d in range(1, half)
+        ]
+        for copy in copies:
+            copy.start()
+        back_recv[which, c, mine] = back_send[which, c, mine]
+        return copies
+
+    def arrived(copies):
+        for copy in copies:
+            copy.wait_recv()
+
+    whole = pl.ds(0, 128)
+    near = [dispatch(near_pick, tokens, 0), dispatch(near_pick, grads, 1)]
+    for copy in locals_:
+        copy.wait()
+    arrived(swaps)
+    arrived(near[0])
+    front_in(0)
+    crossing[0].wait_recv()
+    crossing[1].wait_recv()
+    far = [dispatch(far_pick, far_tok.at[0], 2)]
+    arrived(near[1])
+    front_out(1)
+    pointwise(0)
+    arrived(far[0])
+    front_in(2)
+    crossing[2].wait_recv()
+    far.append(dispatch(far_pick, far_tok.at[1], 3))
+    near_probs = return_probs(0)
+    crossing[3].wait_recv()
+    arrived(far[1])
+    front_out(3)
+    pointwise(1)
+
+    far_back, partials = [], []
+
+    def forward_piece(c):
+        arrived(far_back[c])
+
+        @pl.loop(0, piece // STEP)
+        def _(k):
+            inner = pl.ds(pl.multiple_of(k * STEP, STEP), STEP)
+            rows = rows_of(back_recv.at[1, c], inner)
+            part_send[c, :, inner] = (dot(far_mats[2], rows) + dot(far_mats[3], rows)).astype(
+                jnp.bfloat16
+            )
+
+        copy = remote(part_send.at[c], part_recv.at[c], y_send.at[c], y_recv.at[c], partner)
+        copy.start()
+        partials.append(copy)
+
+    for c in range(PIECES):
+        far_back.append(return_rows(1, c))
+        if c:
+            forward_piece(c - 1)
+    far_probs = return_probs(1)
+    forward_piece(PIECES - 1)
+    arrived(far_probs)
+    far_rows = rows_of(prob_recv.at[1], whole)
+    val_send[0] = dot(far_mats[0], far_rows).astype(jnp.bfloat16)
+    val_send[1] = dot(far_mats[1], far_rows).astype(jnp.bfloat16)
+    values = remote(val_send, val_recv, v_send.at[0], v_recv.at[0], partner)
+    values.start()
+
+    near_back = [return_rows(0, c) for c in range(PIECES)]
+    for c in range(PIECES):
+        arrived(near_back[c])
+        arrived([partials[c]])
+
+        @pl.loop(0, piece // STEP)
+        def _(k):
+            inner = pl.ds(pl.multiple_of(k * STEP, STEP), STEP)
+            rows = rows_of(back_recv.at[0, c], inner)
+            total = dot(near_mats[2], rows) + dot(near_mats[3], rows)
+            total += part_recv[c, :, inner].astype(jnp.float32)
+            cols = pl.ds(pl.multiple_of(c * piece + k * STEP, STEP), STEP)
+            out[:, cols] = total.astype(jnp.bfloat16)
+
+    arrived(near_probs)
+    arrived([values])
+    near_rows = rows_of(prob_recv.at[0], whole)
+    for k in range(2):
+        total = dot(near_mats[k], near_rows) + val_recv[k].astype(jnp.float32)
+        probs_out[k] = total.astype(jnp.bfloat16)
+    groups = [crossing, swaps, *near, *far, near_probs, far_probs, partials, [values]]
+    for copies in groups + far_back + near_back:
+        for copy in copies:
+            copy.wait_send()
+
+
+def fused_on_device(tokens, routes, route_probs, gate_weight, up_weight, down_weight, grad_out):
+    tok_count, width = tokens.shape
+    top_count = routes.shape[1]
+    experts = lax.axis_size("expert")
+    capacity = 3 * tok_count * top_count // (2 * experts)
+    half = experts // 2
+    count = half * capacity
+    hid = gate_weight.shape[2]
+    base = (lax.axis_index("expert") // half) * half
+
+    def tables(first):
+        slots = slots_of(routes, first, half, capacity)
+        lanes = jnp.arange(count, dtype=jnp.int32)[None, None, :]
+        chosen = (slots.T[:, :, None] == lanes).astype(jnp.bfloat16)
+        high, low = weighting_of(slots, route_probs, count)
+        return dispatch_of(slots, count), jnp.concatenate([chosen, jnp.stack([high, low])], axis=0)
+
+    near_pick, near_mats = tables(base)
+    far_pick, far_mats = tables(experts - half - base)
+    vmem, sems = pltpu.VMEM, pltpu.SemaphoreType.DMA
+    bf16 = jnp.bfloat16
+    piece = width // PIECES
+    spec = pl.BlockSpec(memory_space=pltpu.VMEM)
+    raw = pl.BlockSpec(memory_space=pl.ANY)
+    grad_tokens, values = pl.pallas_call(
+        lambda *refs: fused_kernel(half, *refs),
+        name="routed_backward",
+        out_shape=(
+            jax.ShapeDtypeStruct((tok_count, width), bf16),
+            jax.ShapeDtypeStruct((2, tok_count, 128), bf16),
+        ),
+        in_specs=[spec] * 6 + [raw] * 3,
+        out_specs=(spec, spec),
+        scratch_shapes=[
+            vmem((count, tok_count), bf16),
+            vmem((4, tok_count, count), bf16),
+            vmem((2, tok_count, width), bf16),
+            vmem((2, width, hid), bf16),
+            vmem((2, width, hid), bf16),
+            vmem((2, hid, width), bf16),
+            vmem((4, half, capacity, width), bf16),
+            vmem((4, half, capacity, width), bf16),
+            vmem((3, 2, count, hid), jnp.float32),
+            vmem((2, 2, 2, count, hid), bf16),
+            vmem((2, PIECES, half, capacity, piece), bf16),
+            vmem((2, PIECES, half, capacity, piece), bf16),
+            vmem((2, half, capacity, 128), bf16),
+            vmem((2, half, capacity, 128), bf16),
+            vmem((PIECES, tok_count, piece), bf16),
+            vmem((PIECES, tok_count, piece), bf16),
+            vmem((2, tok_count, 128), bf16),
+            vmem((2, tok_count, 128), bf16),
+            sems((3,)),
+            sems((4,)), sems((4,)),
+            sems((3,)), sems((3,)),
+            sems((4, half)), sems((4, half)),
+            sems((2, PIECES, half)), sems((2, PIECES, half)),
+            sems((2, half)), sems((2, half)),
+            sems((PIECES,)), sems((PIECES,)),
+            sems((1,)), sems((1,)),
+        ],
+        compiler_params=pltpu.CompilerParams(
+            collective_id=0, has_side_effects=True, vmem_limit_bytes=63 * 1024 * 1024
+        ),
+    )(
+        tokens, grad_out, near_pick, far_pick, near_mats, far_mats,
+        gate_weight, up_weight, down_weight,
+    )
+    return grad_tokens, values[:, :, 0].T
+
+
+def on_device(tokens, routes, *rest):
+    experts = lax.axis_size("expert")
+    capacity = 3 * routes.shape[0] * routes.shape[1] // (2 * experts)
+    fits = capacity % 8 == 0 and lax.axis_size("seq") == 2 and routes.shape[1] == 2
+    run = fused_on_device if fits else halves_on_device
+    return run(tokens, routes, *rest)
+
+
 def solution(mesh):
     placed = (
         P(("seq", "expert"), None),

time: 301 us -> 246 us (0.82)
  Pallas kernels: 0 us -> 233 us
  waiting for transfers between devices: 148 us -> 0 us
  matrix products: 84 us -> 0 us
  starting transfers between devices: 51.7 us -> 0 us
    pallas_call x0 -> x1, Pallas kernels: none -> 233 us  [fused_on_device(): pl.pallas_call(lambda *refs: fused_kernel(half, *refs), name='routed_back...]
    ppermute x10 -> x0, waiting for transfers between devices: 124 us -> none  [the longest x7 124 us: across(): return lax.ppermute(value, 'expert', swap)]
    dot_general x40 -> x0, matrix products: 84 us -> none  [the longest x20 42.7 us: dot(): return jnp.dot(a, b, preferred_element_type=jnp.float32)]
    all_to_all x8 -> x0, starting transfers between devices: 38 us -> none  [exchange(): lax.all_to_all(value, 'expert', split_axis=0, concat_axis=0, tiled=True,...]
    all_to_all x8 -> x0, waiting for transfers between devices: 23.7 us -> none  [exchange(): lax.all_to_all(value, 'expert', split_axis=0, concat_axis=0, tiled=True,...]
    ppermute x10 -> x0, starting transfers between devices: 13.7 us -> none  [the longest x7 13.2 us: across(): return lax.ppermute(value, 'expert', swap)]
    unnamed x37 -> x2, local copies, waits for them, and re-layouts: 6.07 us -> 3.07 us
  transfers between devices with their start and end apart: 18 -> 0, of which waited for: 8 -> 0; matrix products, arithmetic and copies ran while one was open for 29% -> 0% of each run, Pallas kernels for 0% -> 0%
where the time goes in v1:
time: 246 us; the launch traced here: 245 us
  Pallas kernels  233 us (95%)
  local copies, waits for them, and re-layouts  6.29 us (3%)
  other arithmetic  5.32 us (2%)
    pallas_call x1, Pallas kernels, fused_on_device(): pl.pallas_call(lambda *refs: fused_kernel(half, *refs), name='routed_back...  233 us

profile of v1, /device:TPU:0, one launch (start us, length us, event | category | flops | bytes accessed | tf_op | source)
XLA Modules:
  0.0 245.4 jit_solution(3807204602393727477)
XLA Ops:
  0.6 0.8 copy.19
  1.4 0.1 eq.144
  1.6 0.1 eq.140
  1.7 0.1 eq.133
  1.9 0.1 eq.129
  2.0 0.6 reduce-window.14
  2.6 0.2 slice_reduce_fusion.2
  2.9 0.1 fusion.9
  3.0 0.6 reduce-window.16
  3.6 0.2 slice_reduce_fusion.1
  3.8 0.1 fusion.7
  3.9 0.1 reshape.94
  4.1 0.1 reshape.92
  4.2 0.1 copy.22
  4.3 0.1 copy.20
  4.4 0.1 copy.23
  4.5 0.1 copy.26
  4.6 0.6 convert_element_type.68.refs_2_
  5.3 0.6 convert_element_type.71.refs_3_
  5.9 0.1 fusion.1
  6.0 0.1 fusion
  6.1 0.7 select_reduce_fusion
  6.8 0.1 copy.28
  7.0 0.8 pad_maximum_fusion.1.refs_5_
  7.7 0.1 copy.25
  7.9 0.8 pad_maximum_fusion.refs_4_
  8.6 233.0 %routed_backward.1 = (bf16[128,4096]{1,0:T(8,128)(2,1)}, bf16[2,128,128]{2,1,0:T(8,128)(2,1)}) custom-call(bf16[128,4096]{1,0:T(8,128)(2,1)} %refs_0_.1, bf16[128,4096]{1,0:T(8,128)(2,1)} %refs_1_.1, bf16[192,128]{1,0:T(8,128)(2,1)} %convert_element_type.68.refs_2_, bf16[192,128]{1,0:T(8,128)(2,1)} %convert_element_type.71.refs_3_, ...), custom_call_target="tpu_custom_call" | custom-call | tf_op jit(solution)/shard_map/routed_backward/pallas_call | solution.py:423
  241.7 1.5 slice_reduce_fusion
  243.1 2.3 copy.30
  (12 shorter events, 0.2 us)

commit v2 on v1

--- a/solution.py
+++ b/solution.py
@@ -170,7 +170,7 @@
     capacity = send.shape[2]
     count = half * capacity
     hid = acc.shape[3]
-    piece = width // PIECES
+    piece, middle = width // PIECES, width // 2
     me = lax.axis_index("expert")
     core = lax.axis_index("seq")
     base = (me // half) * half
@@ -204,10 +204,15 @@
     crossing = [
         remote(far_pick_out, far_pick, x_send.at[0], x_recv.at[0], partner),
         remote(tokens, far_tok.at[0], x_send.at[1], x_recv.at[1], partner),
-        remote(grads, far_tok.at[1], x_send.at[2], x_recv.at[2], partner),
-        remote(far_mats_out, far_mats, x_send.at[3], x_recv.at[3], partner),
+        remote(
+            grads.at[:, :middle], far_tok.at[1, :, :middle], x_send.at[2], x_recv.at[2], partner
+        ),
+        remote(
+            grads.at[:, middle:], far_tok.at[1, :, middle:], x_send.at[3], x_recv.at[3], partner
+        ),
+        remote(far_mats_out, far_mats, x_send.at[4], x_recv.at[4], partner),
     ]
-    for copy in crossing:
+    for copy in crossing[:2]:
         copy.start()
     swaps = [
         remote(src.at[0], dst.at[1], w_send.at[i], w_recv.at[i], twin)
@@ -216,8 +221,8 @@
     for copy in swaps:
         copy.start()
 
-    def dispatch(pick, source, stream):
-        @pl.loop(0, width // STEP)
+    def dispatch(pick, source, stream, lane, start, size):
+        @pl.loop(start // STEP, (start + size) // STEP)
         def _(k):
             cols = pl.ds(pl.multiple_of(k * STEP, STEP), STEP)
             rows = dot(pick[...], source[:, cols])
@@ -225,14 +230,16 @@
 
         copies = [
             remote(
-                send.at[stream, peers[d]], recv.at[stream, mine],
-                a_send.at[stream, d], a_recv.at[stream, d], {"expert": base + peers[d]},
+                send.at[stream, peers[d], :, start : start + size],
+                recv.at[stream, mine, :, start : start + size],
+                a_send.at[lane, d], a_recv.at[lane, d], {"expert": base + peers[d]},
             )
             for d in range(1, half)
         ]
         for copy in copies:
             copy.start()
-        recv[stream, mine] = send[stream, mine]
+        own = pl.ds(start, size)
+        recv[stream, mine, :, own] = send[stream, mine, :, own]
         return copies
 
     def rows_of(buffer, cols):
@@ -251,10 +258,11 @@
                 acc[0, j] += dot(rows, gate_w[j, cols, :])
                 acc[1, j] += dot(rows, up_w[j, cols, :])
 
-    def front_out(stream):
-        acc[2] = jnp.zeros(acc.shape[1:], jnp.float32)
-
-        @pl.loop(0, width // STEP)
+    def front_out(stream, start, size):
+        if start == 0:
+            acc[2] = jnp.zeros(acc.shape[1:], jnp.float32)
+
+        @pl.loop(start // STEP, (start + size) // STEP)
         def _(k):
             cols = pl.ds(pl.multiple_of(k * STEP, STEP), STEP)
             rows = rows_of(recv.at[stream], cols)
@@ -318,26 +326,36 @@
             copy.wait_recv()
 
     whole = pl.ds(0, 128)
-    near = [dispatch(near_pick, tokens, 0), dispatch(near_pick, grads, 1)]
+    near = [
+        dispatch(near_pick, tokens, 0, 0, 0, width),
+        dispatch(near_pick, grads, 1, 1, 0, width),
+    ]
+    for copy in crossing[2:]:
+        copy.start()
+    crossing[0].wait_recv()
+    crossing[1].wait_recv()
+    far = [dispatch(far_pick, far_tok.at[0], 2, 2, 0, width)]
     for copy in locals_:
         copy.wait()
     arrived(swaps)
     arrived(near[0])
     front_in(0)
-    crossing[0].wait_recv()
-    crossing[1].wait_recv()
-    far = [dispatch(far_pick, far_tok.at[0], 2)]
     arrived(near[1])
-    front_out(1)
+    front_out(1, 0, width)
     pointwise(0)
+    near_probs = return_probs(0)
+    near_back = [return_rows(0, c) for c in range(PIECES // 2)]
+    crossing[2].wait_recv()
+    far.append(dispatch(far_pick, far_tok.at[1], 3, 3, 0, middle))
     arrived(far[0])
     front_in(2)
-    crossing[2].wait_recv()
-    far.append(dispatch(far_pick, far_tok.at[1], 3))
-    near_probs = return_probs(0)
     crossing[3].wait_recv()
+    far.append(dispatch(far_pick, far_tok.at[1], 3, 4, middle, middle))
+    crossing[4].wait_recv()
     arrived(far[1])
-    front_out(3)
+    front_out(3, 0, middle)
+    arrived(far[2])
+    front_out(3, middle, middle)
     pointwise(1)
 
     far_back, partials = [], []
@@ -370,7 +388,7 @@
     values = remote(val_send, val_recv, v_send.at[0], v_recv.at[0], partner)
     values.start()
 
-    near_back = [return_rows(0, c) for c in range(PIECES)]
+    near_back += [return_rows(0, c) for c in range(PIECES // 2, PIECES)]
     for c in range(PIECES):
         arrived(near_back[c])
         arrived([partials[c]])
@@ -449,9 +467,9 @@
             vmem((2, tok_count, 128), bf16),
             vmem((2, tok_count, 128), bf16),
             sems((3,)),
-            sems((4,)), sems((4,)),
+            sems((5,)), sems((5,)),
             sems((3,)), sems((3,)),
-            sems((4, half)), sems((4, half)),
+            sems((5, half)), sems((5, half)),
             sems((2, PIECES, half)), sems((2, PIECES, half)),
             sems((2, half)), sems((2, half)),
             sems((PIECES,)), sems((PIECES,)),

time: 246 us -> 221 us (0.90)
  Pallas kernels: 233 us -> 209 us
    pallas_call x1, Pallas kernels: 233 us -> 209 us  [fused_on_device(): pl.pallas_call(lambda *refs: fused_kernel(half, *refs), name='routed_back...]
where the time goes in v2:
time: 221 us
  Pallas kernels  209 us (95%)
  local copies, waits for them, and re-layouts  6.29 us (3%)
  other arithmetic  5.32 us (2%)
    pallas_call x1, Pallas kernels, fused_on_device(): pl.pallas_call(lambda *refs: fused_kernel(half, *refs), name='routed_back...  209 us

profile of v2, /device:TPU:0, one launch (start us, length us, event | category | flops | bytes accessed | tf_op | source)
XLA Modules:
  0.0 221.1 jit_solution(1176994600094267401)
XLA Ops:
  0.6 0.8 copy.19
  1.4 0.1 eq.144
  1.6 0.1 eq.140
  1.7 0.1 eq.133
  1.9 0.1 eq.129
  2.0 0.6 reduce-window.14
  2.6 0.2 slice_reduce_fusion.2
  2.9 0.1 fusion.9
  3.0 0.6 reduce-window.16
  3.6 0.2 slice_reduce_fusion.1
  3.8 0.1 fusion.7
  3.9 0.1 reshape.94
  4.1 0.1 reshape.92
  4.2 0.1 copy.22
  4.3 0.1 copy.20
  4.4 0.1 copy.23
  4.5 0.1 copy.26
  4.6 0.6 convert_element_type.68.refs_2_
  5.3 0.6 convert_element_type.71.refs_3_
  5.9 0.1 fusion.1
  6.0 0.1 fusion
  6.1 0.7 select_reduce_fusion
  6.8 0.1 copy.28
  7.0 0.8 pad_maximum_fusion.1.refs_5_
  7.7 0.1 copy.25
  7.9 0.8 pad_maximum_fusion.refs_4_
  8.6 208.7 %routed_backward.1 = (bf16[128,4096]{1,0:T(8,128)(2,1)}, bf16[2,128,128]{2,1,0:T(8,128)(2,1)}) custom-call(bf16[128,4096]{1,0:T(8,128)(2,1)} %refs_0_.1, bf16[128,4096]{1,0:T(8,128)(2,1)} %refs_1_.1, bf16[192,128]{1,0:T(8,128)(2,1)} %convert_element_type.68.refs_2_, bf16[192,128]{1,0:T(8,128)(2,1)} %convert_element_type.71.refs_3_, ...), custom_call_target="tpu_custom_call" | custom-call | tf_op jit(solution)/shard_map/routed_backward/pallas_call | solution.py:441
  217.4 1.5 slice_reduce_fusion
  218.8 2.3 %copy.30 = bf16[128,4096]{1,0:T(8,128)(2,1)} copy(bf16[128,4096]{1,0:T(8,128)(2,1)} %get-tuple-element.18) | data formatting | bytes 2097152
  (12 shorter events, 0.2 us)
